TPU v7x, 128 devices: a whole 4x4x4 slice. The times are simulated.
128 devices in a mesh: section: 8 (over z_hi, y), dp: 16 (over z_lo, x, core).
Axes of the slice: x: 4, y: 4, z: 4 (z_hi: 2, z_lo: 2; z = z_hi * 2 + z_lo), core: 2. Of those that a mesh axis runs over, the one named last changes fastest.
Arguments:
- queries: bfloat16 [8, 32, 128, 4096], P('section', 'dp'), may hold values from -240 to 240, as said below
- image_tokens: bfloat16 [32, 192, 8192], P('dp', 'section'), may hold values from -6 to 6
- key_weight: bfloat16 [8, 8192, 512], P('section'), may hold values from -0.0625 to 0.0625
- value_weight: bfloat16 [8, 8192, 512], P('section'), may hold values from -0.0625 to 0.0625
- cotangent: bfloat16 [8, 32, 128, 4096], P('section', 'dp'), may hold values from -6 to 6
- tile_counts: int32 [32], P('dp'), may hold values from 1 to 4
- text_lengths: int32 [32], P('dp'), may hold values from 32 to 128, as said below
Outputs:
- query_gradient: bfloat16 [8, 32, 128, 4096], P('section', 'dp')
- image_grad: bfloat16 [32, 192, 8192], P('dp', 'section')
- key_weight_grad: bfloat16 [8, 8192, 512], P('section', 'dp')
- value_weight_grad: bfloat16 [8, 8192, 512], P('section', 'dp')
Inputs may be any that keep to these rules, and one draw needn't show every extreme that they name: queries of one row share one scale. `text_lengths`: the live text tokens of a sample come first.
All inputs are finite; a program needn't handle non-finite values.
Results may differ from a plain program's by a relative error of at most 0.025.
The roundings to bfloat16 on the way count: a program that leaves them out, or rounds other values in their place, can miss the bound.
Values may be sent and summed in bfloat16 or wider, within the bound.
A program may use at most 192 MiB of HBM per device.

v0:
```python
import math
import jax
import jax.numpy as jnp
from jax import lax
from jax.sharding import PartitionSpec as P

QUERY_HEADS = 32
KEY_VALUE_HEADS = 4
HEAD_SIZE = 128
MAX_TILES = 4


def attend_one(queries, key_rows, value_rows, cotangent, key_limit, row_limit):
    total_rows = queries.shape[0]
    total_keys = key_rows.shape[0]
    group_width = QUERY_HEADS // KEY_VALUE_HEADS
    heads_of_queries = queries.reshape(total_rows, KEY_VALUE_HEADS, group_width, HEAD_SIZE)
    heads_of_keys = key_rows.reshape(total_keys, KEY_VALUE_HEADS, HEAD_SIZE)
    heads_of_values = value_rows.reshape(total_keys, KEY_VALUE_HEADS, HEAD_SIZE)
    row_live = (jnp.arange(total_rows) < row_limit)[:, None]
    active_cotangent = jnp.where(row_live, cotangent, jnp.zeros_like(cotangent))
    head_gradient = active_cotangent.reshape(total_rows, KEY_VALUE_HEADS, group_width, HEAD_SIZE)
    scaling = 1.0 / math.sqrt(HEAD_SIZE)
    scores = (
        jnp.einsum(
            "lhgd,nhd->hgln", heads_of_queries, heads_of_keys, preferred_element_type=jnp.float32
        )
        * scaling
    )
    key_live = jnp.arange(total_keys) < key_limit
    scores = jnp.where(key_live, scores, -jnp.inf)
    row_max = jnp.max(scores, axis=-1, keepdims=True)
    raised = jnp.exp(scores - row_max)
    weights = raised / jnp.sum(raised, axis=-1, keepdims=True)
    weights_low = weights.astype(jnp.bfloat16)
    value_gradient = jnp.einsum(
        "hgln,lhgd->nhd", weights_low, head_gradient, preferred_element_type=jnp.float32
    ).astype(jnp.bfloat16)
    prob_grad = jnp.einsum(
        "lhgd,nhd->hgln", head_gradient, heads_of_values, preferred_element_type=jnp.float32
    )
    row_dot = jnp.sum(weights * prob_grad, axis=-1, keepdims=True)
    score_grad = (weights * (prob_grad - row_dot) * scaling).astype(jnp.bfloat16)
    query_gradient = jnp.einsum(
        "hgln,nhd->lhgd", score_grad, heads_of_keys, preferred_element_type=jnp.float32
    ).astype(jnp.bfloat16)
    key_gradient = jnp.einsum(
        "hgln,lhgd->nhd", score_grad, heads_of_queries, preferred_element_type=jnp.float32
    ).astype(jnp.bfloat16)
    return (
        query_gradient.reshape(total_rows, QUERY_HEADS * HEAD_SIZE),
        key_gradient.reshape(total_keys, KEY_VALUE_HEADS * HEAD_SIZE),
        value_gradient.reshape(total_keys, KEY_VALUE_HEADS * HEAD_SIZE),
    )


def project(tokens, weight):
    return jnp.dot(tokens, weight, preferred_element_type=jnp.float32).astype(jnp.bfloat16)


def shards(queries, image_tokens, key_weight, value_weight, cotangent, tile_counts, text_lengths):
    gathered = lax.all_gather(image_tokens, "section", axis=1, tiled=True)
    samples_here = gathered.shape[0]
    image_len = gathered.shape[1]
    model_width = gathered.shape[2]
    tile_len = image_len // MAX_TILES
    w_key = key_weight[0]
    w_value = value_weight[0]
    query_local = queries[0]
    cotan_local = cotangent[0]
    query_list = []
    key_list = []
    value_list = []
    flat_tokens = gathered.reshape(samples_here * image_len, model_width)
    keys_all = project(flat_tokens, w_key).reshape(samples_here, image_len, -1)
    values_all = project(flat_tokens, w_value).reshape(samples_here, image_len, -1)
    for sample_index in range(samples_here):
        query_gradient, key_gradient, value_gradient = attend_one(
            query_local[sample_index],
            keys_all[sample_index],
            values_all[sample_index],
            cotan_local[sample_index],
            tile_counts[sample_index] * tile_len,
            text_lengths[sample_index],
        )
        query_list.append(query_gradient)
        key_list.append(key_gradient)
        value_list.append(value_gradient)
    query_out = jnp.stack(query_list)[None]
    key_grads = jnp.stack(key_list)
    value_grads = jnp.stack(value_list)
    image_term = jnp.einsum("stk,dk->std", key_grads, w_key, preferred_element_type=jnp.float32)
    image_term = image_term + jnp.einsum(
        "stk,dk->std", value_grads, w_value, preferred_element_type=jnp.float32
    )
    image_out = lax.psum_scatter(
        image_term.astype(jnp.bfloat16), "section", scatter_dimension=1, tiled=True
    )
    key_term = jnp.einsum("std,stk->dk", gathered, key_grads, preferred_element_type=jnp.float32)
    value_term = jnp.einsum(
        "std,stk->dk", gathered, value_grads, preferred_element_type=jnp.float32
    )
    key_sum, value_sum = (
        lax.psum_scatter(
            key_term.astype(jnp.bfloat16), "dp", scatter_dimension=0, tiled=True
        ).astype(jnp.float32),
        lax.psum_scatter(
            value_term.astype(jnp.bfloat16), "dp", scatter_dimension=0, tiled=True
        ).astype(jnp.float32),
    )
    return (
        query_out,
        image_out,
        key_sum.astype(jnp.bfloat16)[None],
        value_sum.astype(jnp.bfloat16)[None],
    )


def solution(mesh):
    placed = (
        P("section", "dp", None, None),
        P("dp", "section", None),
        P("section", None, None),
        P("section", None, None),
        P("section", "dp", None, None),
        P("dp"),
        P("dp"),
    )
    return jax.shard_map(
        shards,
        mesh=mesh,
        in_specs=placed,
        out_specs=(
            P("section", "dp", None, None),
            P("dp", "section", None),
            P("section", "dp", None),
            P("section", "dp", None),
        ),
        check_vma=False,
    )
```

profile of v0, /device:TPU:0, one launch (start us, length us, event | category | flops | bytes accessed | tf_op | source)
XLA Modules:
  0.0 456.2 jit_solution(1482975594506760739)
XLA Ops:
  18.3 84.2 %all-gather.2.cloned.1.call-done = bf16[2,192,8192]{2,1,0:T(8,128)(2,1)} async-done(((bf16[2,24,8192]{2,1,0:T(8,128)(2,1)}), bf16[2,192,8192]{2,1,0:T(8,128)(2,1)}) %all-gather.2.cloned.1.call-update) | async-done | bytes 6291472 | tf_op jit(solution)/shard_map/all_gather | solution.py:62
  102.4 8.6 %fusion.44 = bf16[384,512]{1,0:T(8,128)(2,1)S(1)} fusion(bf16[384,8192]{1,0:T(8,128)(2,1)} %bitcast.203, bf16[1,8192,512]{2,1,0:T(8,128)(2,1)} %param.10), kind=kOutput, calls=%fused_computation.56 | convolution fusion | flops 3221422080 | bytes 15073280 | tf_op jit(solution)/shard_map/dot_general | solution.py:58
  111.2 8.6 %fusion.41 = bf16[384,512]{1,0:T(8,128)(2,1)S(1)} fusion(bf16[384,8192]{1,0:T(8,128)(2,1)} %bitcast.204, bf16[1,8192,512]{2,1,0:T(8,128)(2,1)} %param.9), kind=kOutput, calls=%fused_computation.55 | convolution fusion | flops 3221422080 | bytes 15073280 | tf_op jit(solution)/shard_map/dot_general | solution.py:58
  123.9 2.3 fusion.72
  126.2 3.7 fusion.116
  129.9 3.4 fusion.68
  133.3 6.6 %fusion.63 = bf16[192,4,128]{2,0,1:T(8,128)(2,1)} fusion(bf16[128,4,8,128]{0,3,2,1:T(8,128)(2,1)S(1)} %bitcast.215, f32[4,192,128,8]{2,1,3,0:T(8,128)} %fusion.72, f32[4,8,128,192]{2,3,1,0:T(8,128)} %get-tuple-element.29, f32[4,8,128]{2,1,0:T(8,128)S(1)} %get-tuple-element.28), kind=kOutput, calls=%fused_computation.65 | convolution fusion | flops 206934208 | bytes 7553024 | tf_op jit(solution)/shard_map/hgln,lhgd->nhd/dot_general | solution.py:47
  142.3 2.4 fusion.71
  144.7 2.7 fusion.121
  147.4 2.7 fusion.65
  150.1 5.7 %fusion.64 = bf16[192,4,128]{2,0,1:T(8,128)(2,1)S(1)} fusion(bf16[128,4,8,128]{0,3,2,1:T(8,128)(2,1)S(1)} %bitcast.213, f32[4,192,128,8]{2,1,3,0:T(8,128)} %fusion.71, f32[4,8,128,192]{2,3,1,0:T(8,128)} %get-tuple-element.31, f32[4,8,128]{2,1,0:T(8,128)S(1)} %get-tuple-element.30), kind=kOutput, calls=%fused_computation.66 | convolution fusion | flops 206934208 | bytes 7553024 | tf_op jit(solution)/shard_map/hgln,lhgd->nhd/dot_general | solution.py:47
  156.6 11.8 %fusion.7 = f32[2,192,8192]{2,1,0:T(8,128)} fusion(bf16[2,192,512]{2,1,0:T(8,128)(2,1)S(1)} %constant_dynamic-update-slice_fusion, bf16[1,8192,512]{2,1,0:T(8,128)(2,1)} %param.9), kind=kOutput, calls=%fused_computation.10 | convolution fusion | flops 3221225472 | bytes 21364736 | tf_op jit(solution)/shard_map/stk,dk->std/dot_general | solution.py:92
  168.3 12.6 %add_convert_fusion = bf16[2,192,8192]{2,1,0:T(8,128)(2,1)} fusion(f32[2,192,8192]{2,1,0:T(8,128)} %fusion.7, bf16[2,192,512]{2,1,0:T(8,128)(2,1)S(1)} %constant_dynamic-update-slice_fusion.2, bf16[1,8192,512]{2,1,0:T(8,128)(2,1)} %param.10), kind=kOutput, calls=%fused_computation.6 | convolution fusion | flops 3227516928 | bytes 27656192 | tf_op jit(solution)/shard_map/stk,dk->std/dot_general | solution.py:93
  180.9 11.1 %copy.93 = bf16[2,192,8192]{2,0,1:T(2,128)(2,1)S(1)} copy(bf16[2,192,8192]{2,1,0:T(8,128)(2,1)} %add_convert_fusion) | data formatting | bytes 12582912
  192.0 6.9 %copy.99 = bf16[24,8,2,8192]{3,1,2,0:T(8,128)(2,1)} copy(bf16[24,8,2,8192]{3,2,1,0:T(2,128)(2,1)S(1)} %bitcast.206) | data formatting | bytes 12582912
  199.0 9.5 %fusion.4 = bf16[8192,512]{0,1:T(8,128)(2,1)} fusion(bf16[2,192,512]{2,1,0:T(8,128)(2,1)S(1)} %constant_dynamic-update-slice_fusion, bf16[2,192,8192]{2,1,0:T(8,128)(2,1)} %all-gather.2.cloned.1.call-done), kind=kOutput, calls=%fused_computation.7 | convolution fusion | flops 3225419776 | bytes 15073280 | tf_op jit(solution)/shard_map/std,stk->dk/dot_general | solution.py:99
  208.6 9.7 %fusion.5 = bf16[8192,512]{0,1:T(8,128)(2,1)} fusion(bf16[2,192,512]{2,1,0:T(8,128)(2,1)S(1)} %constant_dynamic-update-slice_fusion.2, bf16[2,192,8192]{2,1,0:T(8,128)(2,1)} %all-gather.2.cloned.1.call-done), kind=kOutput, calls=%fused_computation.8 | convolution fusion | flops 3225419776 | bytes 15073280 | tf_op jit(solution)/shard_map/std,stk->dk/dot_general | solution.py:100
  219.3 6.1 %convolution_convert_fusion = bf16[4,128,8,128]{3,1,2,0:T(8,128)(2,1)S(1)} fusion(f32[4,192,128,8]{2,1,3,0:T(8,128)} %fusion.72, bf16[192,4,128,1]{2,1,0,3:T(4,128)(2,1)S(1)} %bitcast.225, f32[4,8,128,192]{2,3,1,0:T(8,128)} %get-tuple-element.29, f32[4,8,128]{2,1,0:T(8,128)S(1)} %copy-done.7), kind=kOutput, calls=%fused_computation.49 | convolution fusion | flops 207360192 | bytes 7553024 | tf_op jit(solution)/shard_map/hgln,nhd->lhgd/dot_general | solution.py:44
  225.9 6.4 %convolution_convert_fusion.1 = bf16[4,128,8,128]{3,1,2,0:T(8,128)(2,1)S(1)} fusion(f32[4,192,128,8]{2,1,3,0:T(8,128)} %fusion.71, bf16[192,4,128,1]{2,1,0,3:T(4,128)(2,1)S(1)} %bitcast.223, f32[4,8,128,192]{2,3,1,0:T(8,128)} %get-tuple-element.31, f32[4,8,128]{2,1,0:T(8,128)S(1)} %get-tuple-element.30), kind=kOutput, calls=%fused_computation.50 | convolution fusion | flops 207360192 | bytes 7553024 | tf_op jit(solution)/shard_map/hgln,nhd->lhgd/dot_general | solution.py:44
  234.3 62.0 %reduce-scatter.10.cloned.1.call-done = bf16[24,16384]{1,0:T(8,128)(2,1)} async-done(((bf16[192,16384]{1,0:T(8,128)(2,1)}), bf16[24,16384]{1,0:T(8,128)(2,1)}) %reduce-scatter.10.cloned.1.call-update) | async-done | bytes 786448
  296.3 2.6 reshape.77
  300.2 71.6 %reduce-scatter.6.cloned.1.call-done = bf16[512,512]{0,1:T(8,128)(2,1)} async-done(((bf16[8192,512]{0,1:T(8,128)(2,1)}), bf16[512,512]{0,1:T(8,128)(2,1)}) %reduce-scatter.6.cloned.1.call-update) | async-done | bytes 524304 | tf_op jit(solution)/shard_map/reduce_scatter | solution.py:104
  373.9 73.7 %reduce-scatter.8.cloned.1.call-done = bf16[512,512]{0,1:T(8,128)(2,1)} async-done(((bf16[8192,512]{0,1:T(8,128)(2,1)}), bf16[512,512]{0,1:T(8,128)(2,1)}) %reduce-scatter.8.cloned.1.call-update) | async-done | bytes 524304 | tf_op jit(solution)/shard_map/reduce_scatter | solution.py:107
  447.6 2.0 copy.66
  (59 shorter events, 24.0 us)
Async XLA Ops:
  7.2 95.3 %all-gather.2.cloned.1.call-start = ((), (), s32[]{:S(2)}) async-start(), calls=%async_computation.3 | async-start | bytes 7077888 | tf_op jit(solution)/shard_map/all_gather | solution.py:62
  7.9 288.4 %reduce-scatter.10.cloned.1.call-start = ((), (), s32[]{:S(2)}) async-start(), calls=%async_computation.6 | async-start | bytes 7077888
  13.6 2.0 copy-start
  15.7 0.7 copy-start.5
  119.8 6.4 %copy-start.2 = (bf16[1,1,128,4096]{2,3,1,0:T(8,128)(2,1)S(1)}, bf16[1,1,128,4096]{2,3,1,0:T(8,128)(2,1)}, u32[]{:S(2)}) copy-start(bf16[1,1,128,4096]{2,3,1,0:T(8,128)(2,1)} %copy.96) | copy-start | bytes 3145732
  129.9 3.4 copy-start.6
  139.8 4.8 %copy-start.1 = (bf16[1,1,128,4096]{2,3,1,0:T(8,128)(2,1)S(1)}, bf16[1,1,128,4096]{2,3,1,0:T(8,128)(2,1)}, u32[]{:S(2)}) copy-start(bf16[1,1,128,4096]{2,3,1,0:T(8,128)(2,1)} %copy.95) | copy-start | bytes 3145732
  139.8 4.8 %copy-start.3 = (bf16[192,4,128]{2,1,0:T(4,128)(2,1)S(1)}, bf16[192,4,128]{2,1,0:T(4,128)(2,1)}, u32[]{:S(2)}) copy-start(bf16[192,4,128]{2,1,0:T(4,128)(2,1)} %reshape_squeeze.18) | copy-start | bytes 589828
  198.9 172.9 %reduce-scatter.6.cloned.1.call-start = ((), (), s32[]{:S(2)}) async-start(), calls=%async_computation.4 | async-start | bytes 8912896 | tf_op jit(solution)/shard_map/reduce_scatter | solution.py:104
  208.5 239.1 %reduce-scatter.8.cloned.1.call-start = ((), (), s32[]{:S(2)}) async-start(), calls=%async_computation.5 | async-start | bytes 8912896 | tf_op jit(solution)/shard_map/reduce_scatter | solution.py:107
  218.3 0.9 copy-start.4
  218.3 0.9 copy-start.7
Sparse Core Ops, SparseCore 0:
  10.3 92.1 all-gather.1
  199.0 97.2 reduce-scatter.9
  298.9 72.8 reduce-scatter.5
  374.2 73.3 reduce-scatter.7
where the time goes:
time: 457 us; the launch traced here: 456 us
  waiting for transfers between devices  292 us (64%)
  matrix products  103 us (23%)
  local copies, waits for them, and re-layouts  42.9 us (9%)
  between operations  15.3 us (3%)
    all_gather x1, waiting for transfers between devices, shards(): gathered = lax.all_gather(image_tokens, 'section', axis=1, tiled=True)  84.2 us
    reduce_scatter x1, waiting for transfers between devices, shards(): lax.psum_scatter(value_term.astype(jnp.bfloat16), 'dp', scatter_dimension...  73.7 us
    reduce_scatter x1, waiting for transfers between devices, shards(): lax.psum_scatter(key_term.astype(jnp.bfloat16), 'dp', scatter_dimension=0...  71.6 us
    unnamed x5, waiting for transfers between devices  62.7 us
    unnamed x29, local copies, waits for them, and re-layouts  30.9 us
    dot_general x2, matrix products, project(): jnp.dot(tokens, weight, preferred_element_type=jnp.float32)  17.2 us
    dot_general x1, matrix products, shards(): jnp.einsum('stk,dk->std', value_grads, w_value, preferred_element_type=jn...  12.6 us
    dot_general x2, matrix products, attend_one(): jnp.einsum('hgln,nhd->lhgd', score_grad, heads_of_keys, preferred_element...  12.5 us
  transfers between devices with their start and end apart: 4, of which 4 were waited for; matrix products, arithmetic and copies ran while one was open for 11% of the time, Pallas kernels for 0%

commit v1 on v0

--- a/solution.py
+++ b/solution.py
@@ -8,6 +8,13 @@
 KEY_VALUE_HEADS = 4
 HEAD_SIZE = 128
 MAX_TILES = 4
+
+
+def all_by_exchange(array, axis, dim):
+    size = lax.axis_size(axis)
+    blocks = jnp.stack([array for _ in range(size)])
+    blocks = lax.all_to_all(blocks, axis, split_axis=0, concat_axis=0)
+    return jnp.concatenate(blocks, axis=dim)
 
 
 def attend_one(queries, key_rows, value_rows, cotangent, key_limit, row_limit):
@@ -59,7 +66,7 @@
 
 
 def shards(queries, image_tokens, key_weight, value_weight, cotangent, tile_counts, text_lengths):
-    gathered = lax.all_gather(image_tokens, "section", axis=1, tiled=True)
+    gathered = all_by_exchange(image_tokens, "section", 1)
     samples_here = gathered.shape[0]
     image_len = gathered.shape[1]
     model_width = gathered.shape[2]

time: 457 us -> 473 us (1.035)
  starting transfers between devices: 0.16 us -> 8.12 us
  local copies, waits for them, and re-layouts: 42.9 us -> 49.7 us
    all_gather x1 -> x0, waiting for transfers between devices: 84.2 us -> none  [shards(): gathered = lax.all_gather(image_tokens, 'section', axis=1, tiled=True)]
    all_to_all x0 -> x1, waiting for transfers between devices: none -> 63.8 us  [all_by_exchange(): blocks = lax.all_to_all(blocks, axis, split_axis=0, concat_axis=0)]
    unnamed x5 -> x4, waiting for transfers between devices: 62.7 us -> 84.8 us
    all_to_all x0 -> x1, starting transfers between devices: none -> 8 us  [all_by_exchange(): blocks = lax.all_to_all(blocks, axis, split_axis=0, concat_axis=0)]
    unnamed x29 -> x33, local copies, waits for them, and re-layouts: 30.9 us -> 31 us
  transfers between devices with their start and end apart: 4 -> 4, of which waited for: 4 -> 4; matrix products, arithmetic and copies ran while one was open for 11% -> 10% of each run, Pallas kernels for 0% -> 0%
where the time goes in v1:
time: 473 us
  waiting for transfers between devices  294 us (62%)
  matrix products  103 us (22%)
  local copies, waits for them, and re-layouts  49.7 us (11%)
  between operations  15.3 us (3%)
  starting transfers between devices  8.12 us (2%)
    unnamed x4, waiting for transfers between devices  84.8 us
    reduce_scatter x1, waiting for transfers between devices, shards(): lax.psum_scatter(value_term.astype(jnp.bfloat16), 'dp', scatter_dimension...  73.7 us
    reduce_scatter x1, waiting for transfers between devices, shards(): lax.psum_scatter(key_term.astype(jnp.bfloat16), 'dp', scatter_dimension=0...  71.6 us
    all_to_all x1, waiting for transfers between devices, all_by_exchange(): blocks = lax.all_to_all(blocks, axis, split_axis=0, concat_axis=0)  63.8 us
    unnamed x33, local copies, waits for them, and re-layouts  31 us
    dot_general x2, matrix products, project(): jnp.dot(tokens, weight, preferred_element_type=jnp.float32)  16.9 us
    dot_general x1, matrix products, shards(): jnp.einsum('stk,dk->std', value_grads, w_value, preferred_element_type=jn...  12.8 us
    dot_general x2, matrix products, attend_one(): jnp.einsum('hgln,nhd->lhgd', score_grad, heads_of_keys, preferred_element...  12.4 us
  transfers between devices with their start and end apart: 4, of which 4 were waited for; matrix products, arithmetic and copies ran while one was open for 10% of the time, Pallas kernels for 0%

profile of v1, /device:TPU:0, one launch (start us, length us, event | category | flops | bytes accessed | tf_op | source)
XLA Modules:
  0.0 472.5 jit_solution(7471263317103301857)
XLA Ops:
  7.2 4.5 stack.8
  11.7 8.0 %all-to-all-start = ((bf16[8,2,24,8192]{3,2,1,0:T(8,128)(2,1)}), bf16[8,2,24,8192]{3,2,1,0:T(8,128)(2,1)}, u32[]{:S(2)}, u32[]{:S(2)}) async-start(bf16[8,2,24,8192]{3,2,1,0:T(8,128)(2,1)} %stack.8), calls=%async_computation | async-start | bytes 12582912 | tf_op jit(solution)/shard_map/all_to_all | solution.py:16
  29.4 63.8 %all-to-all-done = bf16[8,2,24,8192]{3,2,1,0:T(8,128)(2,1)} async-done(((bf16[8,2,24,8192]{3,2,1,0:T(8,128)(2,1)}), bf16[8,2,24,8192]{3,2,1,0:T(8,128)(2,1)}, u32[]{:S(2)}, u32[]{:S(2)}) %all-to-all-start) | async-done | bytes 6291488 | tf_op jit(solution)/shard_map/all_to_all | solution.py:16
  93.2 3.2 copy.68
  96.4 8.3 %fusion.44 = bf16[384,512]{1,0:T(8,128)(2,1)S(1)} fusion(bf16[384,8192]{1,0:T(8,128)(2,1)S(1)} %bitcast.207, bf16[1,8192,512]{2,1,0:T(8,128)(2,1)} %param.10), kind=kOutput, calls=%fused_computation.56 | convolution fusion | flops 3221422080 | bytes 15073280 | tf_op jit(solution)/shard_map/dot_general | solution.py:65
  104.8 8.6 %fusion.41 = bf16[384,512]{1,0:T(8,128)(2,1)S(1)} fusion(bf16[384,8192]{1,0:T(8,128)(2,1)} %bitcast.208, bf16[1,8192,512]{2,1,0:T(8,128)(2,1)} %param.9), kind=kOutput, calls=%fused_computation.55 | convolution fusion | flops 3221422080 | bytes 15073280 | tf_op jit(solution)/shard_map/dot_general | solution.py:65
  119.9 3.7 fusion.116
  123.5 3.4 fusion.68
  126.9 6.6 %fusion.63 = bf16[192,4,128]{2,0,1:T(8,128)(2,1)} fusion(bf16[128,4,8,128]{0,3,2,1:T(8,128)(2,1)S(1)} %bitcast.221, f32[4,192,128,8]{2,1,3,0:T(8,128)} %fusion.72, f32[4,8,128,192]{2,3,1,0:T(8,128)} %get-tuple-element.33, f32[4,8,128]{2,1,0:T(8,128)S(1)} %get-tuple-element.32), kind=kOutput, calls=%fused_computation.65 | convolution fusion | flops 206934208 | bytes 7553024 | tf_op jit(solution)/shard_map/hgln,lhgd->nhd/dot_general | solution.py:54
  138.3 2.7 fusion.121
  141.0 2.7 fusion.65
  143.7 5.7 %fusion.64 = bf16[192,4,128]{2,0,1:T(8,128)(2,1)S(1)} fusion(bf16[128,4,8,128]{0,3,2,1:T(8,128)(2,1)S(1)} %bitcast.219, f32[4,192,128,8]{2,1,3,0:T(8,128)} %fusion.71, f32[4,8,128,192]{2,3,1,0:T(8,128)} %get-tuple-element.35, f32[4,8,128]{2,1,0:T(8,128)S(1)} %get-tuple-element.34), kind=kOutput, calls=%fused_computation.66 | convolution fusion | flops 206934208 | bytes 7553024 | tf_op jit(solution)/shard_map/hgln,lhgd->nhd/dot_general | solution.py:54
  150.0 11.8 %fusion.7 = f32[2,192,8192]{2,1,0:T(8,128)} fusion(bf16[2,192,512]{2,1,0:T(8,128)(2,1)S(1)} %constant_dynamic-update-slice_fusion, bf16[1,8192,512]{2,1,0:T(8,128)(2,1)} %param.9), kind=kOutput, calls=%fused_computation.10 | convolution fusion | flops 3221225472 | bytes 21364736 | tf_op jit(solution)/shard_map/stk,dk->std/dot_general | solution.py:99
  161.8 12.8 %add_convert_fusion = bf16[2,192,8192]{2,1,0:T(8,128)(2,1)} fusion(f32[2,192,8192]{2,1,0:T(8,128)} %fusion.7, bf16[2,192,512]{2,1,0:T(8,128)(2,1)S(1)} %constant_dynamic-update-slice_fusion.2, bf16[1,8192,512]{2,1,0:T(8,128)(2,1)} %param.10), kind=kOutput, calls=%fused_computation.6 | convolution fusion | flops 3227516928 | bytes 27656192 | tf_op jit(solution)/shard_map/stk,dk->std/dot_general | solution.py:100
  174.6 11.1 %copy.117 = bf16[2,192,8192]{2,0,1:T(2,128)(2,1)S(1)} copy(bf16[2,192,8192]{2,1,0:T(8,128)(2,1)} %add_convert_fusion) | data formatting | bytes 12582912
  185.7 6.9 %copy.123 = bf16[24,8,2,8192]{3,1,2,0:T(8,128)(2,1)} copy(bf16[24,8,2,8192]{3,2,1,0:T(2,128)(2,1)S(1)} %bitcast.212) | data formatting | bytes 12582912
  192.7 9.5 %fusion.4 = bf16[8192,512]{0,1:T(8,128)(2,1)} fusion(bf16[2,192,512]{2,1,0:T(8,128)(2,1)S(1)} %constant_dynamic-update-slice_fusion, bf16[2,192,8192]{2,1,0:T(8,128)(2,1)} %bitcast.209), kind=kOutput, calls=%fused_computation.7 | convolution fusion | flops 3225419776 | bytes 15073280 | tf_op jit(solution)/shard_map/std,stk->dk/dot_general | solution.py:106
  202.3 9.8 %fusion.5 = bf16[8192,512]{0,1:T(8,128)(2,1)} fusion(bf16[2,192,512]{2,1,0:T(8,128)(2,1)S(1)} %constant_dynamic-update-slice_fusion.2, bf16[2,192,8192]{2,1,0:T(8,128)(2,1)} %bitcast.210), kind=kOutput, calls=%fused_computation.8 | convolution fusion | flops 3225419776 | bytes 15073280 | tf_op jit(solution)/shard_map/std,stk->dk/dot_general | solution.py:107
  213.0 6.0 %convolution_convert_fusion = bf16[4,128,8,128]{3,1,2,0:T(8,128)(2,1)S(1)} fusion(f32[4,192,128,8]{2,1,3,0:T(8,128)} %fusion.72, bf16[192,4,128,1]{2,1,0,3:T(4,128)(2,1)S(1)} %bitcast.231, f32[4,8,128,192]{2,3,1,0:T(8,128)} %get-tuple-element.33, f32[4,8,128]{2,1,0:T(8,128)S(1)} %copy-done.9), kind=kOutput, calls=%fused_computation.49 | convolution fusion | flops 207360192 | bytes 7553024 | tf_op jit(solution)/shard_map/hgln,nhd->lhgd/dot_general | solution.py:51
  219.5 6.4 %convolution_convert_fusion.1 = bf16[4,128,8,128]{3,1,2,0:T(8,128)(2,1)S(1)} fusion(f32[4,192,128,8]{2,1,3,0:T(8,128)} %fusion.71, bf16[192,4,128,1]{2,1,0,3:T(4,128)(2,1)S(1)} %bitcast.229, f32[4,8,128,192]{2,3,1,0:T(8,128)} %get-tuple-element.35, f32[4,8,128]{2,1,0:T(8,128)S(1)} %get-tuple-element.34), kind=kOutput, calls=%fused_computation.50 | convolution fusion | flops 207360192 | bytes 7553024 | tf_op jit(solution)/shard_map/hgln,nhd->lhgd/dot_general | solution.py:51
  228.0 84.8 %reduce-scatter.10.cloned.1.call-done = bf16[24,16384]{1,0:T(8,128)(2,1)} async-done(((bf16[192,16384]{1,0:T(8,128)(2,1)}), bf16[24,16384]{1,0:T(8,128)(2,1)}) %reduce-scatter.10.cloned.1.call-update) | async-done | bytes 786448
  312.7 2.6 reshape.83
  316.6 71.6 %reduce-scatter.6.cloned.1.call-done = bf16[512,512]{0,1:T(8,128)(2,1)} async-done(((bf16[8192,512]{0,1:T(8,128)(2,1)}), bf16[512,512]{0,1:T(8,128)(2,1)}) %reduce-scatter.6.cloned.1.call-update) | async-done | bytes 524304 | tf_op jit(solution)/shard_map/reduce_scatter | solution.py:111
  390.2 73.7 %reduce-scatter.8.cloned.1.call-done = bf16[512,512]{0,1:T(8,128)(2,1)} async-done(((bf16[8192,512]{0,1:T(8,128)(2,1)}), bf16[512,512]{0,1:T(8,128)(2,1)}) %reduce-scatter.8.cloned.1.call-update) | async-done | bytes 524304 | tf_op jit(solution)/shard_map/reduce_scatter | solution.py:114
  (64 shorter events, 29.2 us)
Async XLA Ops:
  11.7 8.0 %copy-start.6 = (s32[2]{0:T(128)S(1)}, s32[2]{0:T(128)}, u32[]{:S(2)}) copy-start(s32[2]{0:T(128)} %param.12) | copy-start | bytes 28
  11.7 81.5 %all-to-all-start = ((bf16[8,2,24,8192]{3,2,1,0:T(8,128)(2,1)}), bf16[8,2,24,8192]{3,2,1,0:T(8,128)(2,1)}, u32[]{:S(2)}, u32[]{:S(2)}) async-start(bf16[8,2,24,8192]{3,2,1,0:T(8,128)(2,1)} %stack.8), calls=%async_computation | async-start | bytes 12582912 | tf_op jit(solution)/shard_map/all_to_all | solution.py:16
  19.7 293.1 %reduce-scatter.10.cloned.1.call-start = ((), (), s32[]{:S(2)}) async-start(), calls=%async_computation.6 | async-start | bytes 7077888
  24.7 2.0 copy-start.1
  26.8 0.7 copy-start.7
  96.4 8.3 %copy-start = (bf16[8,2,24,8192]{3,2,0,1:T(8,128)(2,1)}, bf16[8,2,24,8192]{3,2,0,1:T(8,128)(2,1)S(1)}, u32[]{:S(2)}) copy-start(bf16[8,2,24,8192]{3,2,0,1:T(8,128)(2,1)S(1)} %copy.68) | copy-start | bytes 18874372
  113.5 6.4 %copy-start.3 = (bf16[1,1,128,4096]{2,3,1,0:T(8,128)(2,1)S(1)}, bf16[1,1,128,4096]{2,3,1,0:T(8,128)(2,1)}, u32[]{:S(2)}) copy-start(bf16[1,1,128,4096]{2,3,1,0:T(8,128)(2,1)} %copy.120) | copy-start | bytes 3145732
  123.5 3.4 copy-start.8
  133.5 4.8 %copy-start.2 = (bf16[1,1,128,4096]{2,3,1,0:T(8,128)(2,1)S(1)}, bf16[1,1,128,4096]{2,3,1,0:T(8,128)(2,1)}, u32[]{:S(2)}) copy-start(bf16[1,1,128,4096]{2,3,1,0:T(8,128)(2,1)} %copy.119) | copy-start | bytes 3145732
  133.5 4.8 %copy-start.4 = (bf16[192,4,128]{2,1,0:T(4,128)(2,1)S(1)}, bf16[192,4,128]{2,1,0:T(4,128)(2,1)}, u32[]{:S(2)}) copy-start(bf16[192,4,128]{2,1,0:T(4,128)(2,1)} %reshape_squeeze.18) | copy-start | bytes 589828
  192.6 195.6 %reduce-scatter.6.cloned.1.call-start = ((), (), s32[]{:S(2)}) async-start(), calls=%async_computation.4 | async-start | bytes 8912896 | tf_op jit(solution)/shard_map/reduce_scatter | solution.py:111
  202.2 261.7 %reduce-scatter.8.cloned.1.call-start = ((), (), s32[]{:S(2)}) async-start(), calls=%async_computation.5 | async-start | bytes 8912896 | tf_op jit(solution)/shard_map/reduce_scatter | solution.py:114
  212.1 0.9 copy-start.5
  212.1 0.9 copy-start.9
Sparse Core Ops, SparseCore 0:
  192.7 119.9 reduce-scatter.9
  315.3 72.8 reduce-scatter.5
  390.7 73.1 reduce-scatter.7
